TPU v7x, 256 devices: a whole 4x4x8 slice. The times are simulated.
256 devices in a mesh: row: 32 (over z, y_lo, core), col: 8 (over y_hi, x).
Axes of the slice: x: 4, y: 4 (y_hi: 2, y_lo: 2; y = y_hi * 2 + y_lo), z: 8, core: 2. Of those that a mesh axis runs over, the one named last changes fastest.
Arguments:
- matrix: float32 [14336, 14336], P('row', 'col'), may hold values from -16 to 16, as said below
- panels: float32 [2, 14336, 128], P(None, 'row'), may hold values from -0.050111484 to 0.050111484
- factors: float32 [2, 128, 128], replicated, may hold values from -1.2 to 1.6, as said below
Outputs:
- updated: float32 [14336, 14336], P('row', 'col')
Inputs may be any that keep to these rules, and one draw needn't show every extreme that they name: symmetric: matrix[r, c] equals matrix[c, r]. Each factors[p] is upper triangular, with diagonal entries between 0.8 and 1.6.
All inputs are finite; a program needn't handle non-finite values.
Results may differ from a plain program's by a relative error of at most 0.0001.
Values sent between devices are 32-bit elements; how exact they have to be, the bound alone decides.
A program may use at most 64 MiB of HBM per device.

v0:
```python
import jax
import jax.numpy as jnp
from jax import lax
from jax.sharding import PartitionSpec as P


def matmul(former, latter):
    return jnp.dot(former, latter, precision=lax.Precision.HIGHEST)


def transposed_dot(former, latter):
    return lax.dot_general(
        former, latter, (((0,), (0,)), ((), ())), precision=lax.Precision.HIGHEST
    )


def outer_drop(current, former, latter):
    return current - lax.dot_general(
        former, latter, (((1,), (1,)), ((), ())), precision=lax.Precision.HIGHEST
    )


def weights(forward, vectors, factor, correct):
    return matmul(forward, factor) - 0.5 * matmul(vectors, correct)


def row_sums(current, vector_rows, extra_terms):
    summed = lax.psum((transposed_dot(current, vector_rows),) + extra_terms, "row")
    return (summed[0], tuple(summed[1:]))


def shards(matrix, panels, factors):
    col_index = lax.axis_index("col")
    local_cols = matrix.shape[1]
    gathered = lax.all_gather(panels, "row", axis=1, tiled=True)
    vector_cols = lax.dynamic_slice_in_dim(gathered, col_index * local_cols, local_cols, 1)
    current = matrix
    for number in range(panels.shape[0]):
        vector_rows = panels[number]
        vcol_now = vector_cols[number]
        factor = factors[number]
        forward = lax.psum(matmul(current, vcol_now), "col")
        forward_cols, summed = row_sums(
            current, vector_rows, (transposed_dot(vector_rows, forward),)
        )
        correct = matmul(factor.T, matmul(summed[0], factor))
        wrow_now = weights(forward, vector_rows, factor, correct)
        wcol_now = weights(forward_cols, vcol_now, factor, correct)
        current = outer_drop(
            current,
            jnp.concatenate([vector_rows, wrow_now], axis=1),
            jnp.concatenate([wcol_now, vcol_now], axis=1),
        )
    return current


def solution(mesh):
    placed = (P("row", "col"), P(None, "row", None), P())
    return jax.shard_map(
        shards, mesh=mesh, in_specs=placed, out_specs=P("row", "col"), check_vma=False
    )
```

profile of v0, /device:TPU:1, one launch (start us, length us, event | category | flops | bytes accessed | tf_op | source)
XLA Modules:
  0.0 775.0 jit_solution(1958344349460214117)
XLA Ops:
  6.5 0.7 all-gather.2.cloned.1.call-update
  7.3 95.2 %all-gather.2.cloned.1.call-done = f32[2,14336,128]{2,1,0:T(8,128)} async-done(((f32[2,448,128]{2,1,0:T(8,128)}), f32[2,14336,128]{2,1,0:T(8,128)}) %all-gather.2.cloned.1.call-update) | async-done | bytes 14680080 | tf_op jit(solution)/shard_map/all_gather | solution.py:35
  102.5 2.5 dynamic-slice_bitcast_fusion
  105.0 0.9 copy-done.3
  105.9 3.4 convolution_bitcast_fusion
  109.3 0.0 all-reduce.13.cloned.1.call-start
  109.4 7.8 %fusion.44 = f32[1792,128]{1,0:T(8,128)} fusion(f32[448,1792]{1,0:T(8,128)S(1)} %copy-done, f32[2,448,128]{2,1,0:T(8,128)} %param.4), kind=kOutput, calls=%fused_computation.57 | convolution fusion | flops 1233125376 | bytes 4358144 | tf_op jit(solution)/shard_map/dot_general | solution.py:12
  117.2 74.7 %all-reduce.7.cloned.1.call-done = f32[448,128]{1,0:T(8,128)} async-done(((f32[448,128]{1,0:T(8,128)}), f32[448,128]{1,0:T(8,128)}) %all-reduce.7.cloned.1.call-update) | async-done | bytes 229392 | tf_op jit(solution)/shard_map/psum | solution.py:42
  191.9 2.3 convolution_bitcast_fusion.2
  194.2 0.2 all-reduce.9.cloned.1.call-start
  194.4 1.9 slice_bitcast_fusion
  196.3 1.3 fusion.32
  197.6 228.8 %all-reduce.13.cloned.1.call-done = (f32[1792,128]{1,0:T(8,128)}, f32[128,128]{0,1:T(8,128)}) async-done(((f32[1792,128]{1,0:T(8,128)}, f32[128,128]{0,1:T(8,128)}), (f32[1792,128]{1,0:T(8,128)}, f32[128,128]{0,1:T(8,128)})) %all-reduce.13.cloned.1.call-update) | async-done | bytes 983056 | tf_op jit(solution)/shard_map/psum | solution.py:28
  426.3 2.1 fusion.26
  428.4 1.1 fusion.30
  429.6 0.3 fusion.28
  429.9 0.9 fusion.1
  430.8 0.4 fusion.11
  431.2 5.1 convolution_subtract_fusion.1
  436.3 3.4 fusion.46
  439.7 0.3 all-reduce.11.cloned.1.call-start
  439.9 7.8 %fusion.45 = f32[1792,128]{1,0:T(8,128)} fusion(f32[448,1792]{1,0:T(8,128)S(1)} %convolution_subtract_fusion.1, f32[2,448,128]{2,1,0:T(8,128)} %param.4), kind=kOutput, calls=%fused_computation.58 | convolution fusion | flops 1233125376 | bytes 4358144 | tf_op jit(solution)/shard_map/dot_general | solution.py:12
  447.7 75.9 %all-reduce.9.cloned.1.call-done = f32[448,128]{1,0:T(8,128)} async-done(((f32[448,128]{1,0:T(8,128)}), f32[448,128]{1,0:T(8,128)}) %all-reduce.9.cloned.1.call-update) | async-done | bytes 229392 | tf_op jit(solution)/shard_map/psum | solution.py:42
  523.6 2.3 convolution_bitcast_fusion.1
  525.9 2.0 fusion.24
  527.9 230.0 %all-reduce.11.cloned.1.call-done = (f32[1792,128]{1,0:T(8,128)}, f32[128,128]{0,1:T(8,128)}) async-done(((f32[1792,128]{1,0:T(8,128)}, f32[128,128]{0,1:T(8,128)}), (f32[1792,128]{1,0:T(8,128)}, f32[128,128]{0,1:T(8,128)})) %all-reduce.11.cloned.1.call-update) | async-done | bytes 983056 | tf_op jit(solution)/shard_map/psum | solution.py:28
  757.9 2.2 fusion.18
  760.1 1.1 fusion.22
  761.2 0.3 fusion.20
  761.5 2.1 fusion
  763.6 0.4 fusion.9
  764.0 4.5 convolution_subtract_fusion
  (27 shorter events, 0.2 us)
Async XLA Ops:
  6.5 99.4 %copy-start = (f32[448,1792]{1,0:T(8,128)S(1)}, f32[448,1792]{1,0:T(8,128)}, u32[]{:S(2)}) copy-start(f32[448,1792]{1,0:T(8,128)} %param.3) | copy-start | bytes 9633796
  6.5 96.0 %all-gather.2.cloned.1.call-start = ((), (), s32[]{:S(2)}) async-start(), calls=%async_computation | async-start | bytes 15138816 | tf_op jit(solution)/shard_map/all_gather | solution.py:35
  7.3 184.6 %all-reduce.7.cloned.1.call-start = ((), (), s32[]{:S(2)}) async-start(), calls=%async_computation.1 | async-start | bytes 458752 | tf_op jit(solution)/shard_map/psum | solution.py:42
  105.0 0.9 copy-start.3
  109.3 87.0 %copy-start.7 = (f32[2,128,128]{2,1,0:T(8,128)S(1)}, f32[2,128,128]{2,1,0:T(8,128)}, u32[]{:S(2)}) copy-start(f32[2,128,128]{2,1,0:T(8,128)} %param.5) | copy-start | bytes 393220
  109.3 317.0 %all-reduce.13.cloned.1.call-start = ((), (), s32[]{:S(2)}) async-start(), calls=%async_computation.4 | async-start | bytes 1966080 | tf_op jit(solution)/shard_map/psum | solution.py:28
  117.2 312.7 %copy-start.4 = (f32[1792,128]{1,0:T(8,128)S(1)}, f32[1792,128]{1,0:T(8,128)}, u32[]{:S(2)}) copy-start(f32[1792,128]{1,0:T(8,128)} %copy-done.3) | copy-start | bytes 2752516
  194.2 236.6 %copy-start.5 = (f32[2,448,128]{2,1,0:T(8,128)S(1)}, f32[2,448,128]{2,1,0:T(8,128)}, u32[]{:S(2)}) copy-start(f32[2,448,128]{2,1,0:T(8,128)} %param.4) | copy-start | bytes 1376260
  194.2 329.4 %all-reduce.9.cloned.1.call-start = ((), (), s32[]{:S(2)}) async-start(), calls=%async_computation.2 | async-start | bytes 458752 | tf_op jit(solution)/shard_map/psum | solution.py:42
  426.3 4.8 copy-start.9
  431.2 5.1 copy-start.1
  439.7 318.2 %all-reduce.11.cloned.1.call-start = ((), (), s32[]{:S(2)}) async-start(), calls=%async_computation.3 | async-start | bytes 1966080 | tf_op jit(solution)/shard_map/psum | solution.py:28
  757.9 5.7 copy-start.6
  757.9 5.7 copy-start.10
  757.9 6.1 copy-start.2
  757.9 6.1 copy-start.8
Sparse Core Ops, SparseCore 0:
  9.1 93.3 all-gather.1
  109.4 82.4 all-reduce.6
  194.6 231.7 all-reduce.12
  439.8 83.7 all-reduce.8
  526.2 231.7 all-reduce.10
where the time goes:
time: 775 us
  waiting for transfers between devices  705 us (91%)
  matrix products  50.4 us (7%)
  between operations  13.3 us (2%)
    psum x2, waiting for transfers between devices, row_sums(): lax.psum((transposed_dot(current, vector_rows),) + extra_terms, 'row')  459 us
    psum x2, waiting for transfers between devices, shards(): forward = lax.psum(matmul(current, vcol_now), 'col')  151 us
    all_gather x1, waiting for transfers between devices, shards(): gathered = lax.all_gather(panels, 'row', axis=1, tiled=True)  95.2 us
    dot_general x14, matrix products, matmul(): return jnp.dot(former, latter, precision=lax.Precision.HIGHEST)  20.8 us
    dot_general x4, matrix products, transposed_dot(): lax.dot_general(former, latter, (((0,), (0,)), ((), ())), precision=lax.P...  20.1 us
  transfers between devices with their start and end apart: 5, of which 5 were waited for; matrix products, arithmetic and copies ran while one was open for 3% of the time, Pallas kernels for 0%

commit v1 on v0

--- a/solution.py
+++ b/solution.py
@@ -32,7 +32,7 @@
 def shards(matrix, panels, factors):
     col_index = lax.axis_index("col")
     local_cols = matrix.shape[1]
-    gathered = lax.all_gather(panels, "row", axis=1, tiled=True)
+    gathered = jnp.concatenate(lax.all_gather(panels, "row"), axis=1)
     vector_cols = lax.dynamic_slice_in_dim(gathered, col_index * local_cols, local_cols, 1)
     current = matrix
     for number in range(panels.shape[0]):

time: 775 us -> 788 us (1.017)
  local copies, waits for them, and re-layouts: 5.37 us -> 22.4 us
    reshape x0 -> x1, local copies, waits for them, and re-layouts: none -> 12.1 us  [shards(): gathered = jnp.concatenate(lax.all_gather(panels, 'row'), axis=1)]
where the time goes in v1:
time: 788 us; the launch traced here: 787 us
  waiting for transfers between devices  702 us (89%)
  matrix products  49.6 us (6%)
  local copies, waits for them, and re-layouts  22.4 us (3%)
  between operations  13.3 us (2%)
    psum x2, waiting for transfers between devices, row_sums(): lax.psum((transposed_dot(current, vector_rows),) + extra_terms, 'row')  455 us
    psum x2, waiting for transfers between devices, shards(): forward = lax.psum(matmul(current, vcol_now), 'col')  151 us
    all_gather x1, waiting for transfers between devices, shards(): gathered = jnp.concatenate(lax.all_gather(panels, 'row'), axis=1)  95.2 us
    dot_general x4, matrix products, transposed_dot(): lax.dot_general(former, latter, (((0,), (0,)), ((), ())), precision=lax.P...  20.2 us
    dot_general x14, matrix products, matmul(): return jnp.dot(former, latter, precision=lax.Precision.HIGHEST)  20.1 us
  transfers between devices with their start and end apart: 5, of which 5 were waited for; matrix products, arithmetic and copies ran while one was open for 3% of the time, Pallas kernels for 0%

profile of v1, /device:TPU:1, one launch (start us, length us, event | category | flops | bytes accessed | tf_op | source)
XLA Modules:
  0.0 787.4 jit_solution(1272126847037757994)
XLA Ops:
  6.5 0.7 all-gather.3.cloned.1.call-update
  7.3 95.2 %all-gather.3.cloned.1.call-done = f32[64,448,128]{2,1,0:T(8,128)} async-done(((f32[2,448,128]{2,1,0:T(8,128)}), f32[64,448,128]{2,1,0:T(8,128)}) %all-gather.3.cloned.1.call-update) | async-done | bytes 14680080 | tf_op jit(solution)/shard_map/all_gather | solution.py:35
  102.6 12.1 %copy.6 = f32[2,32,448,128]{3,2,1,0:T(8,128)} copy(f32[2,32,448,128]{3,2,0,1:T(8,128)} %bitcast.79) | data formatting | bytes 29360128 | tf_op jit(solution)/shard_map/reshape | solution.py:35
  114.6 2.6 constant_dynamic-slice_fusion.1
  117.3 0.9 copy-done.2
  118.2 3.4 convolution_bitcast_fusion
  121.7 7.8 fusion.49
  129.5 74.7 %all-reduce.7.cloned.1.call-done = f32[448,128]{1,0:T(8,128)} async-done(((f32[448,128]{1,0:T(8,128)}), f32[448,128]{1,0:T(8,128)}) %all-reduce.7.cloned.1.call-update) | async-done | bytes 229392 | tf_op jit(solution)/shard_map/psum | solution.py:42
  204.1 2.3 convolution_bitcast_fusion.2
  206.7 1.9 slice_bitcast_fusion
  208.6 2.4 copy.9
  211.0 0.3 fusion.37
  211.3 227.3 %all-reduce.13.cloned.1.call-done = (f32[1792,128]{1,0:T(8,128)}, f32[128,128]{0,1:T(8,128)}) async-done(((f32[1792,128]{1,0:T(8,128)}, f32[128,128]{0,1:T(8,128)}), (f32[1792,128]{1,0:T(8,128)}, f32[128,128]{0,1:T(8,128)})) %all-reduce.13.cloned.1.call-update) | async-done | bytes 983056 | tf_op jit(solution)/shard_map/psum | solution.py:28
  438.6 2.2 fusion.31
  440.8 1.1 fusion.35
  441.9 0.3 fusion.33
  442.2 0.9 fusion.1
  443.2 0.4 fusion.11
  443.6 4.9 convolution_subtract_fusion.1
  448.5 3.4 fusion.13
  452.2 7.8 fusion.50
  460.0 76.0 %all-reduce.9.cloned.1.call-done = f32[448,128]{1,0:T(8,128)} async-done(((f32[448,128]{1,0:T(8,128)}), f32[448,128]{1,0:T(8,128)}) %all-reduce.9.cloned.1.call-update) | async-done | bytes 229392 | tf_op jit(solution)/shard_map/psum | solution.py:42
  535.9 2.3 convolution_bitcast_fusion.1
  538.2 2.4 copy.10
  540.6 2.0 fusion.29
  542.6 227.6 %all-reduce.11.cloned.1.call-done = (f32[1792,128]{1,0:T(8,128)}, f32[128,128]{0,1:T(8,128)}) async-done(((f32[1792,128]{1,0:T(8,128)}, f32[128,128]{0,1:T(8,128)}), (f32[1792,128]{1,0:T(8,128)}, f32[128,128]{0,1:T(8,128)})) %all-reduce.11.cloned.1.call-update) | async-done | bytes 983056 | tf_op jit(solution)/shard_map/psum | solution.py:28
  770.2 2.3 fusion.23
  772.5 1.1 fusion.27
  773.6 0.3 fusion.25
  773.9 2.1 fusion
  776.1 0.4 fusion.9
  776.4 4.4 convolution_subtract_fusion
  (32 shorter events, 0.7 us)
Async XLA Ops:
  6.5 96.0 %all-gather.3.cloned.1.call-start = ((), (), s32[]{:S(2)}) async-start(), calls=%async_computation.2 | async-start | bytes 15138816 | tf_op jit(solution)/shard_map/all_gather | solution.py:35
  7.3 196.9 %all-reduce.7.cloned.1.call-start = ((), (), s32[]{:S(2)}) async-start(), calls=%async_computation | async-start | bytes 458752 | tf_op jit(solution)/shard_map/psum | solution.py:42
  114.6 3.6 copy-start
  117.3 0.9 copy-start.2
  121.6 317.0 %all-reduce.13.cloned.1.call-start = ((), (), s32[]{:S(2)}) async-start(), calls=%async_computation.4 | async-start | bytes 1966080 | tf_op jit(solution)/shard_map/psum | solution.py:28
  129.5 81.5 %copy-start.8 = (f32[2,128,128]{2,1,0:T(8,128)S(1)}, f32[2,128,128]{2,1,0:T(8,128)}, u32[]{:S(2)}) copy-start(f32[2,128,128]{2,1,0:T(8,128)} %param.5) | copy-start | bytes 393220
  204.1 6.9 copy-start.10
  206.4 235.8 %copy-start.3 = (f32[1,1792,128]{2,1,0:T(8,128)S(1)}, f32[1,1792,128]{2,1,0:T(8,128)}, u32[]{:S(2)}) copy-start(f32[1,1792,128]{2,1,0:T(8,128)} %copy-done.2) | copy-start | bytes 2752516
  206.5 329.5 %all-reduce.9.cloned.1.call-start = ((), (), s32[]{:S(2)}) async-start(), calls=%async_computation.1 | async-start | bytes 458752 | tf_op jit(solution)/shard_map/psum | solution.py:42
  211.0 232.2 %copy-start.4 = (f32[2,448,128]{2,1,0:T(8,128)S(1)}, f32[2,448,128]{2,1,0:T(8,128)}, u32[]{:S(2)}) copy-start(f32[2,448,128]{2,1,0:T(8,128)} %param.4) | copy-start | bytes 1376260
  438.6 5.0 copy-start.7
  443.6 4.9 copy-start.1
  451.9 318.3 %all-reduce.11.cloned.1.call-start = ((), (), s32[]{:S(2)}) async-start(), calls=%async_computation.3 | async-start | bytes 1966080 | tf_op jit(solution)/shard_map/psum | solution.py:28
  770.2 5.8 copy-start.5
  770.2 5.8 copy-start.11
  770.2 6.2 copy-start.6
  770.2 6.2 copy-start.9
Sparse Core Ops, SparseCore 0:
  9.2 93.3 all-gather.2
  121.7 82.3 all-reduce.6
  206.8 231.7 all-reduce.12
  452.0 83.8 all-reduce.8
  538.5 231.7 all-reduce.10
